TPU v7x, 256 devices: a whole 4x4x8 slice. The times are simulated.
256 devices in a mesh: dp: 16 (over z, core), tensor: 4 (over y), corpus: 4 (over x).
Axes of the slice: x: 4, y: 4, z: 8, core: 2. Of those that a mesh axis runs over, the one named last changes fastest.
Arguments:
- queries: bfloat16 [4096, 2048], P(('dp', 'tensor', 'corpus')), may hold values from -24 to 24
- passages: bfloat16 [65536, 2048], P(('dp', 'corpus'), 'tensor'), may hold values from -6 to 6
- pos_ids: int32 [4096], P(('dp', 'tensor', 'corpus')), may hold values from 0 to 65535, as said below
- neg_ids: int32 [4096, 32], P(('dp', 'tensor', 'corpus')), may hold values from 0 to 65535, as said below
Outputs:
- grad_query: float32 [4096, 2048], P(('dp', 'tensor', 'corpus'))
- losses: float32 [4096], P(('dp', 'tensor', 'corpus'))
- grad_pass: float32 [65536, 2048], P(('dp', 'corpus'), 'tensor')
Inputs may be any that keep to these rules, and one draw needn't show every extreme that they name: `pos_ids`: together with neg_ids: the ids named by the 16 queries of one device, positives and negatives together, fall at most 16 times into one block of 1024 passage rows (rows b * 1024 to (b + 1) * 1024 - 1), and exactly 16 times into one block that is the same for every device. Ids may repeat. `neg_ids`: counted together with pos_ids as stated there.
All inputs are finite; a program needn't handle non-finite values.
Results may differ from a plain program's by a relative error of at most 0.0035.
Values may be sent and summed in bfloat16 or wider, within the bound.
A program may use at most 128 MiB of HBM per device.

v0:
```python
import jax
import jax.numpy as jnp
from jax import lax
from jax.sharding import PartitionSpec as P


def lookup_rows(row_table, asked_ids):
    return jnp.take(row_table, asked_ids, axis=0, mode="fill", fill_value=0)


def body(queries, passages, pos_ids, neg_ids):
    per_device, feat_width = queries.shape
    block_rows, shard_width = passages.shape
    neg_count = neg_ids.shape[1]
    owners = lax.axis_size("dp") * lax.axis_size("corpus")
    slot_count = 2 * per_device * (neg_count + 1) // owners
    score_scale = feat_width ** (-0.5)
    wanted = jnp.concatenate([pos_ids[:, None], neg_ids], axis=1).reshape(-1)
    owner_of = wanted // block_rows
    local_row = wanted % block_rows
    matches = (owner_of[:, None] == jnp.arange(owners)[None, :]).astype(jnp.int32)
    earlier = jnp.cumsum(matches, axis=0) - matches
    slot_of = owner_of * slot_count + jnp.sum(earlier * matches, axis=1)
    send_ids = jnp.full((owners * slot_count,), block_rows, jnp.int32).at[slot_of].set(local_row)
    send_ids = send_ids.reshape(owners, slot_count)
    row_table = lax.all_gather(passages, "tensor", axis=1, tiled=True)
    asked_ids = lax.all_to_all(send_ids, ("dp", "corpus"), split_axis=0, concat_axis=0, tiled=True)
    found = lookup_rows(row_table, asked_ids)
    fetched = lax.all_to_all(found, ("dp", "corpus"), split_axis=0, concat_axis=0, tiled=True)
    gathered = fetched.reshape(owners * slot_count, feat_width)[slot_of]
    gathered = gathered.reshape(per_device, neg_count + 1, feat_width)
    pos_rows = gathered[:, 0, :]
    neg_rows = gathered[:, 1:, :]
    in_batch = lax.all_gather(pos_rows, "dp", axis=0, tiled=True)
    columns = in_batch.shape[0]
    in_scores = (
        lax.dot_general(
            queries, in_batch, (((1,), (1,)), ((), ())), preferred_element_type=jnp.float32
        )
        * score_scale
    )
    neg_scores = (
        jnp.einsum("md,mkd->mk", queries, neg_rows, preferred_element_type=jnp.float32)
        * score_scale
    )
    logits = jnp.concatenate([in_scores, neg_scores], axis=1)
    row_max = jnp.max(logits, axis=1, keepdims=True)
    exponent = jnp.exp(logits - row_max)
    denominator = jnp.sum(exponent, axis=1, keepdims=True)
    own_col = lax.axis_index("dp") * per_device + jnp.arange(per_device)
    target = (jnp.arange(columns + neg_count)[None, :] == own_col[:, None]).astype(jnp.float32)
    losses = jnp.log(denominator[:, 0]) + row_max[:, 0] - jnp.sum(target * logits, axis=1)
    weights = (exponent / denominator - target).astype(jnp.bfloat16)
    in_weights = weights[:, :columns]
    neg_weights = weights[:, columns:]
    grad_query = jnp.dot(in_weights, in_batch, preferred_element_type=jnp.float32)
    grad_query = grad_query + jnp.einsum(
        "mk,mkd->md", neg_weights, neg_rows, preferred_element_type=jnp.float32
    )
    grad_query = grad_query * score_scale
    in_terms = lax.dot_general(
        in_weights, queries, (((0,), (0,)), ((), ())), preferred_element_type=jnp.float32
    )
    pos_grad = lax.psum_scatter(in_terms, "dp", scatter_dimension=0, tiled=True) * score_scale
    neg_grad = (
        neg_weights.astype(jnp.float32)[:, :, None]
        * queries.astype(jnp.float32)[:, None, :]
        * score_scale
    )
    row_grads = jnp.concatenate([pos_grad[:, None, :], neg_grad], axis=1).astype(jnp.bfloat16)
    row_grads = row_grads.reshape(-1, feat_width)
    grad_slots = (
        jnp.zeros((owners * slot_count, feat_width), jnp.bfloat16).at[slot_of].set(row_grads)
    )
    grad_slots = grad_slots.reshape(owners, slot_count, feat_width)
    arrived = lax.all_to_all(grad_slots, ("dp", "corpus"), split_axis=0, concat_axis=0, tiled=True)
    accum_grad = jnp.zeros((block_rows, feat_width), jnp.float32)
    accum_grad = accum_grad.at[asked_ids.reshape(-1)].add(
        arrived.reshape(-1, feat_width).astype(jnp.float32), mode="drop"
    )
    grad_pass = lax.psum_scatter(accum_grad, "tensor", scatter_dimension=1, tiled=True)
    return (grad_query, losses, grad_pass)


def solution(mesh):
    in_specs = (
        P(("dp", "tensor", "corpus"), None),
        P(("dp", "corpus"), "tensor"),
        P(("dp", "tensor", "corpus")),
        P(("dp", "tensor", "corpus"), None),
    )
    out_specs = (
        P(("dp", "tensor", "corpus"), None),
        P(("dp", "tensor", "corpus")),
        P(("dp", "corpus"), "tensor"),
    )
    return jax.shard_map(body, mesh=mesh, in_specs=in_specs, out_specs=out_specs, check_vma=False)
```

profile of v0, /device:TPU:1, one launch (start us, length us, event | category | flops | bytes accessed | tf_op | source)
XLA Modules:
  0.0 520.4 jit_solution(17081883421997860384)
XLA Ops:
  9.7 1.5 reduce-window.6
  11.7 4.1 scatter_custom_fusion
  15.8 22.0 %all_to_all.25 = s32[64,1,16]{2,1,0:T(1,128)S(1)} all-to-all(s32[64,1,16]{2,1,0:T(1,128)S(1)} %bitcast.53), channel_id=1, replica_groups=mesh['dp'=16,'tensor'=4,'corpus'=4] {'dp','corpus'}, dimensions={0} | all-to-all | bytes 8192 | tf_op jit(solution)/shard_map/all_to_all | solution.py:27
  37.9 26.3 %all-gather.4.cloned.1.call-done = bf16[1024,2048]{1,0:T(8,128)(2,1)} async-done(((bf16[1024,512]{1,0:T(8,128)(2,1)}), bf16[1024,2048]{1,0:T(8,128)(2,1)}) %all-gather.4.cloned.1.call-update) | async-done | bytes 4194320 | tf_op jit(solution)/shard_map/all_gather | solution.py:26
  64.2 11.6 %gather_fusion = bf16[1024,2048]{1,0:T(8,128)(2,1)} fusion(bf16[1024,2048]{1,0:T(8,128)(2,1)} %all-gather.4.cloned.1.call-done, s32[1024]{0:T(1024)S(1)} %broadcast_clamp_fusion), kind=kCustom, calls=%fused_computation | custom fusion | bytes 8392704 | tf_op jit(solution)/shard_map/jit(_take)/gather | solution.py:8
  75.8 4.5 broadcast_select_fusion
  80.3 11.0 %all-to-all-start.1 = ((bf16[64,16,2048]{2,1,0:T(8,128)(2,1)}), bf16[64,16,2048]{2,1,0:T(8,128)(2,1)}, u32[]{:S(2)}, u32[]{:S(2)}) async-start(bf16[64,16,2048]{2,1,0:T(8,128)(2,1)} %broadcast_select_fusion), calls=%async_computation.1 | async-start | bytes 8388608 | tf_op jit(solution)/shard_map/all_to_all | solution.py:29
  91.4 93.5 %all-to-all-done.1 = bf16[64,16,2048]{2,1,0:T(8,128)(2,1)} async-done(((bf16[64,16,2048]{2,1,0:T(8,128)(2,1)}), bf16[64,16,2048]{2,1,0:T(8,128)(2,1)}, u32[]{:S(2)}, u32[]{:S(2)}) %all-to-all-start.1) | async-done | bytes 4194336 | tf_op jit(solution)/shard_map/all_to_all | solution.py:29
  184.9 9.0 %gather_fusion.1 = bf16[528,2048]{1,0:T(8,128)(2,1)S(1)} fusion(bf16[1024,2048]{1,0:T(8,128)(2,1)} %bitcast.6, s32[1024]{0:T(1024)S(1)} %pad_clamp_fusion), kind=kCustom, calls=%fused_computation.1 | custom fusion | bytes 4327488 | tf_op jit(solution)/shard_map/gather | solution.py:30
  193.9 1.9 reshape.222
  197.8 2.4 fusion.8
  200.4 34.0 %all-gather.6.cloned.1.call-done = bf16[256,1,2048]{2,0,1:T(8,128)(2,1)} async-done(((bf16[16,1,2048]{2,0,1:T(8,128)(2,1)}), bf16[256,1,2048]{2,0,1:T(8,128)(2,1)}) %all-gather.6.cloned.1.call-update) | async-done | bytes 1048592 | tf_op jit(solution)/shard_map/all_gather | solution.py:34
  234.4 1.7 fusion.27
  236.4 1.8 fusion.18
  238.2 1.8 multiply_convert_fusion
  240.1 53.7 %reduce-scatter.3.cloned.1.call-done = f32[16,2048]{1,0:T(8,128)} async-done(((f32[256,2048]{1,0:T(8,128)}), f32[16,2048]{1,0:T(8,128)}) %reduce-scatter.3.cloned.1.call-update) | async-done | bytes 131088 | tf_op jit(solution)/shard_map/reduce_scatter | solution.py:64
  294.8 2.4 pad_maximum_fusion
  297.2 1.8 reshape.255
  299.0 10.4 %scatter_custom_fusion.1 = bf16[1024,2048]{1,0:T(8,128)(2,1)} fusion(s32[528]{0:T(1024)S(1)} %fusion.23, bf16[528,2048]{1,0:T(8,128)(2,1)} %reshape.255, bf16[]{:T(256)} %constant.66.clone.1), kind=kCustom, calls=%fused_computation.13 | custom fusion | bytes 4194816 | tf_op jit(solution)/shard_map/scatter | solution.py:73
  309.4 10.7 %all-to-all-start.2 = ((bf16[64,16,2048]{2,1,0:T(8,128)(2,1)}), bf16[64,16,2048]{2,1,0:T(8,128)(2,1)}, u32[]{:S(2)}, u32[]{:S(2)}) async-start(bf16[64,16,2048]{2,1,0:T(8,128)(2,1)} %bitcast.46), calls=%async_computation.3 | async-start | bytes 8388608 | tf_op jit(solution)/shard_map/all_to_all | solution.py:76
  321.7 91.9 %all-to-all-done.2 = bf16[64,16,2048]{2,1,0:T(8,128)(2,1)} async-done(((bf16[64,16,2048]{2,1,0:T(8,128)(2,1)}), bf16[64,16,2048]{2,1,0:T(8,128)(2,1)}, u32[]{:S(2)}, u32[]{:S(2)}) %all-to-all-start.2) | async-done | bytes 4194336 | tf_op jit(solution)/shard_map/all_to_all | solution.py:76
  413.7 18.3 %scatter_custom_fusion.2 = f32[1024,2048]{1,0:T(8,128)} fusion(s32[1024]{0:T(1024)S(1)} %bitcast.56, bf16[1024,2048]{1,0:T(8,128)(2,1)} %bitcast.18, f32[]{:T(128)} %constant.69.clone.1), kind=kCustom, calls=%fused_computation.5 | custom fusion | flops 4194304 | bytes 12582916 | tf_op jit(solution)/shard_map/scatter-add | solution.py:78
  432.6 2.4 fusion.6
  435.8 78.0 %reduce-scatter.5.cloned.1.call-done = f32[1024,512]{1,0:T(8,128)} async-done(((f32[1024,2048]{1,0:T(8,128)}), f32[1024,512]{1,0:T(8,128)}) %reduce-scatter.5.cloned.1.call-update) | async-done | bytes 2097168 | tf_op jit(solution)/shard_map/reduce_scatter | solution.py:81
  (47 shorter events, 9.7 us)
Async XLA Ops:
  7.2 57.1 %all-gather.4.cloned.1.call-start = ((), (), s32[]{:S(2)}) async-start(), calls=%async_computation.5 | async-start | bytes 5242880 | tf_op jit(solution)/shard_map/all_gather | solution.py:26
  80.3 104.6 %all-to-all-start.1 = ((bf16[64,16,2048]{2,1,0:T(8,128)(2,1)}), bf16[64,16,2048]{2,1,0:T(8,128)(2,1)}, u32[]{:S(2)}, u32[]{:S(2)}) async-start(bf16[64,16,2048]{2,1,0:T(8,128)(2,1)} %broadcast_select_fusion), calls=%async_computation.1 | async-start | bytes 8388608 | tf_op jit(solution)/shard_map/all_to_all | solution.py:29
  91.3 143.0 %all-gather.6.cloned.1.call-start = ((), (), s32[]{:S(2)}) async-start(), calls=%async_computation.8 | async-start | bytes 1114112 | tf_op jit(solution)/shard_map/all_gather | solution.py:34
  193.9 3.9 copy-start.1
  197.6 96.2 %reduce-scatter.3.cloned.1.call-start = ((), (), s32[]{:S(2)}) async-start(), calls=%async_computation.6 | async-start | bytes 2228224 | tf_op jit(solution)/shard_map/reduce_scatter | solution.py:64
  309.4 104.3 %all-to-all-start.2 = ((bf16[64,16,2048]{2,1,0:T(8,128)(2,1)}), bf16[64,16,2048]{2,1,0:T(8,128)(2,1)}, u32[]{:S(2)}, u32[]{:S(2)}) async-start(bf16[64,16,2048]{2,1,0:T(8,128)(2,1)} %bitcast.46), calls=%async_computation.3 | async-start | bytes 8388608 | tf_op jit(solution)/shard_map/all_to_all | solution.py:76
  320.1 193.7 %reduce-scatter.5.cloned.1.call-start = ((), (), s32[]{:S(2)}) async-start(), calls=%async_computation.7 | async-start | bytes 10485760 | tf_op jit(solution)/shard_map/reduce_scatter | solution.py:81
  432.0 2.9 copy-start
Sparse Core Ops, SparseCore 0:
  9.8 54.3 all-gather.3
  197.7 36.6 all-gather.5
  238.3 55.4 reduce-scatter.2
  432.2 81.6 reduce-scatter.4
where the time goes:
time: 521 us; the launch traced here: 520 us
  waiting for transfers between devices  378 us (73%)
  local copies, waits for them, and re-layouts  42.5 us (8%)
  other arithmetic  32.2 us (6%)
  starting transfers between devices  22.3 us (4%)
  blocking collectives  22 us (4%)
  between operations  14 us (3%)
  matrix products  9.2 us (2%)
    all_to_all x1, waiting for transfers between devices, body(): lax.all_to_all(found, ('dp', 'corpus'), split_axis=0, concat_axis=0, tile...  93.5 us
    all_to_all x1, waiting for transfers between devices, body(): lax.all_to_all(grad_slots, ('dp', 'corpus'), split_axis=0, concat_axis=0,...  91.9 us
    reduce_scatter x1, waiting for transfers between devices, body(): lax.psum_scatter(accum_grad, 'tensor', scatter_dimension=1, tiled=True)  78 us
    reduce_scatter x1, waiting for transfers between devices, body(): lax.psum_scatter(in_terms, 'dp', scatter_dimension=0, tiled=True)  53.7 us
    all_gather x1, waiting for transfers between devices, body(): in_batch = lax.all_gather(pos_rows, 'dp', axis=0, tiled=True)  34 us
    all_gather x1, waiting for transfers between devices, body(): row_table = lax.all_gather(passages, 'tensor', axis=1, tiled=True)  26.3 us
    all_to_all x1, blocking collectives, body(): lax.all_to_all(send_ids, ('dp', 'corpus'), split_axis=0, concat_axis=0, t...  22 us
    scatter-add x1, other arithmetic, body(): accum_grad.at[asked_ids.reshape(-1)]  18.3 us
  transfers between devices with their start and end apart: 6, of which 6 were waited for; matrix products, arithmetic and copies ran while one was open for 3% of the time, Pallas kernels for 0%

commit v1 on v0

--- a/solution.py
+++ b/solution.py
@@ -2,6 +2,12 @@
 import jax.numpy as jnp
 from jax import lax
 from jax.sharding import PartitionSpec as P
+
+
+def in_order(blocks, dim):
+    blocks = jnp.moveaxis(blocks, 0, dim)
+    shape = blocks.shape
+    return blocks.reshape(*shape[:dim], shape[dim] * shape[dim + 1], *shape[dim + 2 :])
 
 
 def lookup_rows(row_table, asked_ids):
@@ -23,7 +29,19 @@
     slot_of = owner_of * slot_count + jnp.sum(earlier * matches, axis=1)
     send_ids = jnp.full((owners * slot_count,), block_rows, jnp.int32).at[slot_of].set(local_row)
     send_ids = send_ids.reshape(owners, slot_count)
-    row_table = lax.all_gather(passages, "tensor", axis=1, tiled=True)
+    size = lax.axis_size("tensor")
+    pairs = [(i, (i + 1) % size) for i in range(size)]
+    back = [(b, a) for a, b in pairs]
+    lower, upper = ([], [])
+    for step in range(size - 1):
+        if step % 2 == 0:
+            lower.append(lax.ppermute(lower[-1] if lower else passages, "tensor", pairs))
+        else:
+            upper.append(lax.ppermute(upper[-1] if upper else passages, "tensor", back))
+    tiles = jnp.stack([*lower[::-1], passages, *upper])
+    shift = lax.axis_index("tensor") - len(lower)
+    tiles = tiles[(jnp.arange(size) - shift) % size]
+    row_table = in_order(tiles, 1)
     asked_ids = lax.all_to_all(send_ids, ("dp", "corpus"), split_axis=0, concat_axis=0, tiled=True)
     found = lookup_rows(row_table, asked_ids)
     fetched = lax.all_to_all(found, ("dp", "corpus"), split_axis=0, concat_axis=0, tiled=True)

time: 521 us -> 530 us (1.017)
  blocking collectives: 22 us -> 0 us
  starting transfers between devices: 22.3 us -> 40.9 us
  local copies, waits for them, and re-layouts: 42.5 us -> 52.9 us
    all_gather x1 -> x0, waiting for transfers between devices: 26.3 us -> none  [body(): row_table = lax.all_gather(passages, 'tensor', axis=1, tiled=True)]
    all_to_all x1 -> x0, blocking collectives: 22 us -> none  [body(): lax.all_to_all(send_ids, ('dp', 'corpus'), split_axis=0, concat_axis=0, t...]
    ppermute x0 -> x3, waiting for transfers between devices: none -> 17.5 us  [the longest x2 17.5 us: body(): lax.ppermute(lower[-1] if lower else passages, 'tensor', pairs)]
    all_to_all x0 -> x1, starting transfers between devices: none -> 13.4 us  [body(): lax.all_to_all(send_ids, ('dp', 'corpus'), split_axis=0, concat_axis=0, t...]
    all_to_all x0 -> x1, waiting for transfers between devices: none -> 9.08 us  [body(): lax.all_to_all(send_ids, ('dp', 'corpus'), split_axis=0, concat_axis=0, t...]
  transfers between devices with their start and end apart: 6 -> 9, of which waited for: 6 -> 7; matrix products, arithmetic and copies ran while one was open for 3% -> 3% of each run, Pallas kernels for 0% -> 0%
where the time goes in v1:
time: 530 us; the launch traced here: 529 us
  waiting for transfers between devices  377 us (71%)
  local copies, waits for them, and re-layouts  52.9 us (10%)
  starting transfers between devices  40.9 us (8%)
  other arithmetic  35.5 us (7%)
  between operations  14 us (3%)
  matrix products  9.2 us (2%)
    all_to_all x1, waiting for transfers between devices, body(): lax.all_to_all(found, ('dp', 'corpus'), split_axis=0, concat_axis=0, tile...  93.3 us
    all_to_all x1, waiting for transfers between devices, body(): lax.all_to_all(grad_slots, ('dp', 'corpus'), split_axis=0, concat_axis=0,...  92.2 us
    reduce_scatter x1, waiting for transfers between devices, body(): lax.psum_scatter(accum_grad, 'tensor', scatter_dimension=1, tiled=True)  78 us
    reduce_scatter x1, waiting for transfers between devices, body(): lax.psum_scatter(in_terms, 'dp', scatter_dimension=0, tiled=True)  53.7 us
    all_gather x1, waiting for transfers between devices, body(): in_batch = lax.all_gather(pos_rows, 'dp', axis=0, tiled=True)  32.8 us
    scatter-add x1, other arithmetic, body(): accum_grad.at[asked_ids.reshape(-1)]  18.3 us
    ppermute x2, waiting for transfers between devices, body(): lax.ppermute(lower[-1] if lower else passages, 'tensor', pairs)  17.5 us
    all_to_all x1, starting transfers between devices, body(): lax.all_to_all(send_ids, ('dp', 'corpus'), split_axis=0, concat_axis=0, t...  13.4 us
  transfers between devices with their start and end apart: 9, of which 7 were waited for; matrix products, arithmetic and copies ran while one was open for 3% of the time, Pallas kernels for 0%

profile of v1, /device:TPU:1, one launch (start us, length us, event | category | flops | bytes accessed | tf_op | source)
XLA Modules:
  0.0 529.1 jit_solution(5606218844857086565)
XLA Ops:
  7.2 2.2 collective-permute-start
  14.5 17.5 %collective-permute-done = bf16[1024,512]{1,0:T(8,128)(2,1)S(1)} collective-permute-done((bf16[1024,512]{1,0:T(8,128)(2,1)}, bf16[1024,512]{1,0:T(8,128)(2,1)S(1)}, u32[]{:S(2)}, u32[]{:S(2)}) %collective-permute-start) | collective-permute-done | bytes 1048608 | tf_op jit(solution)/shard_map/ppermute | solution.py:38
  33.6 4.1 scatter_custom_fusion
  38.4 13.4 %all-to-all-start = ((s32[64,1,16]{2,1,0:T(1,128)}), s32[64,1,16]{2,1,0:T(1,128)S(1)}, u32[]{:S(2)}, u32[]{:S(2)}) async-start(s32[64,1,16]{2,1,0:T(1,128)} %bitcast.2), calls=%async_computation | async-start | bytes 65536 | tf_op jit(solution)/shard_map/all_to_all | solution.py:45
  51.9 9.1 %all-to-all-done = s32[64,1,16]{2,1,0:T(1,128)S(1)} async-done(((s32[64,1,16]{2,1,0:T(1,128)}), s32[64,1,16]{2,1,0:T(1,128)S(1)}, u32[]{:S(2)}, u32[]{:S(2)}) %all-to-all-start) | async-done | bytes 4128 | tf_op jit(solution)/shard_map/all_to_all | solution.py:45
  61.1 3.3 pad_maximum_fusion
  64.4 4.9 gather_fusion
  69.3 4.8 copy.28
  74.1 11.6 %gather_fusion.1 = bf16[1024,2048]{1,0:T(8,128)(2,1)} fusion(bf16[1024,2048]{1,0:T(8,128)(2,1)} %bitcast.55, s32[1024]{0:T(1024)S(1)} %broadcast_clamp_fusion), kind=kCustom, calls=%fused_computation.1 | custom fusion | bytes 8392704 | tf_op jit(solution)/shard_map/jit(_take)/gather | solution.py:14
  85.7 4.5 broadcast_select_fusion
  90.2 11.0 %all-to-all-start.1 = ((bf16[64,16,2048]{2,1,0:T(8,128)(2,1)}), bf16[64,16,2048]{2,1,0:T(8,128)(2,1)}, u32[]{:S(2)}, u32[]{:S(2)}) async-start(bf16[64,16,2048]{2,1,0:T(8,128)(2,1)} %broadcast_select_fusion), calls=%async_computation.1 | async-start | bytes 8388608 | tf_op jit(solution)/shard_map/all_to_all | solution.py:47
  101.4 93.3 %all-to-all-done.1 = bf16[64,16,2048]{2,1,0:T(8,128)(2,1)} async-done(((bf16[64,16,2048]{2,1,0:T(8,128)(2,1)}), bf16[64,16,2048]{2,1,0:T(8,128)(2,1)}, u32[]{:S(2)}, u32[]{:S(2)}) %all-to-all-start.1) | async-done | bytes 4194336 | tf_op jit(solution)/shard_map/all_to_all | solution.py:47
  194.7 9.0 %gather_fusion.2 = bf16[528,2048]{1,0:T(8,128)(2,1)S(1)} fusion(bf16[1024,2048]{1,0:T(8,128)(2,1)} %bitcast.12, s32[1024]{0:T(1024)S(1)} %pad_clamp_fusion), kind=kCustom, calls=%fused_computation.2 | custom fusion | bytes 4327488 | tf_op jit(solution)/shard_map/gather | solution.py:48
  203.8 1.9 reshape.275
  207.5 2.4 fusion.8
  210.1 32.8 %all-gather.3.cloned.1.call-done = bf16[256,1,2048]{2,0,1:T(8,128)(2,1)} async-done(((bf16[16,1,2048]{2,0,1:T(8,128)(2,1)}), bf16[256,1,2048]{2,0,1:T(8,128)(2,1)}) %all-gather.3.cloned.1.call-update) | async-done | bytes 1048592 | tf_op jit(solution)/shard_map/all_gather | solution.py:52
  248.5 53.7 %reduce-scatter.3.cloned.1.call-done = f32[16,2048]{1,0:T(8,128)} async-done(((f32[256,2048]{1,0:T(8,128)}), f32[16,2048]{1,0:T(8,128)}) %reduce-scatter.3.cloned.1.call-update) | async-done | bytes 131088 | tf_op jit(solution)/shard_map/reduce_scatter | solution.py:82
  303.3 2.4 pad_maximum_fusion.1
  307.4 10.4 %scatter_custom_fusion.1 = bf16[1024,2048]{1,0:T(8,128)(2,1)} fusion(s32[528]{0:T(1024)S(1)} %fusion.23, bf16[528,2048]{1,0:T(8,128)(2,1)} %reshape.316, bf16[]{:T(256)} %constant.90.clone.1), kind=kCustom, calls=%fused_computation.15 | custom fusion | bytes 4194816 | tf_op jit(solution)/shard_map/scatter | solution.py:91
  317.8 11.0 %all-to-all-start.2 = ((bf16[64,16,2048]{2,1,0:T(8,128)(2,1)}), bf16[64,16,2048]{2,1,0:T(8,128)(2,1)}, u32[]{:S(2)}, u32[]{:S(2)}) async-start(bf16[64,16,2048]{2,1,0:T(8,128)(2,1)} %bitcast.56), calls=%async_computation.3 | async-start | bytes 8388608 | tf_op jit(solution)/shard_map/all_to_all | solution.py:94
  330.2 92.2 %all-to-all-done.2 = bf16[64,16,2048]{2,1,0:T(8,128)(2,1)} async-done(((bf16[64,16,2048]{2,1,0:T(8,128)(2,1)}), bf16[64,16,2048]{2,1,0:T(8,128)(2,1)}, u32[]{:S(2)}, u32[]{:S(2)}) %all-to-all-start.2) | async-done | bytes 4194336 | tf_op jit(solution)/shard_map/all_to_all | solution.py:94
  422.3 18.3 %scatter_custom_fusion.2 = f32[1024,2048]{1,0:T(8,128)} fusion(s32[1024]{0:T(1024)S(1)} %bitcast.70, bf16[1024,2048]{1,0:T(8,128)(2,1)} %bitcast.24, f32[]{:T(128)} %constant.93.clone.1), kind=kCustom, calls=%fused_computation.6 | custom fusion | flops 4194304 | bytes 12582916 | tf_op jit(solution)/shard_map/scatter-add | solution.py:96
  441.2 2.4 fusion.6
  444.5 78.0 %reduce-scatter.5.cloned.1.call-done = f32[1024,512]{1,0:T(8,128)} async-done(((f32[1024,2048]{1,0:T(8,128)}), f32[1024,512]{1,0:T(8,128)}) %reduce-scatter.5.cloned.1.call-update) | async-done | bytes 2097168 | tf_op jit(solution)/shard_map/reduce_scatter | solution.py:99
  (56 shorter events, 21.0 us)
Async XLA Ops:
  7.2 24.8 %collective-permute-start = (bf16[1024,512]{1,0:T(8,128)(2,1)}, bf16[1024,512]{1,0:T(8,128)(2,1)S(1)}, u32[]{:S(2)}, u32[]{:S(2)}) collective-permute-start(bf16[1024,512]{1,0:T(8,128)(2,1)} %param.5), channel_id=1, source_target_pairs={{0,4},{4,8},{8,12},{12,0},{1,5},{5,9},{9,13},{13,1},{2,6},{6,10},{... | collective-permute-start | bytes 3145736 | tf_op jit(solution)/shard_map/ppermute | solution.py:38
  9.4 51.8 %collective-permute-start.2 = (bf16[1024,512]{1,0:T(8,128)(2,1)}, bf16[1024,512]{1,0:T(8,128)(2,1)S(1)}, u32[]{:S(2)}, u32[]{:S(2)}) collective-permute-start(bf16[1024,512]{1,0:T(8,128)(2,1)} %param.5), channel_id=1, source_target_pairs={{4,0},{8,4},{12,8},{0,12},{5,1},{9,5},{13,9},{1,13},{6,2},{10,6},{... | collective-permute-start | bytes 3145736 | tf_op jit(solution)/shard_map/ppermute | solution.py:40
  31.9 29.2 %collective-permute-start.1 = (bf16[1024,512]{1,0:T(8,128)(2,1)S(1)}, bf16[1024,512]{1,0:T(8,128)(2,1)S(1)}, u32[]{:S(2)}, u32[]{:S(2)}) collective-permute-start(bf16[1024,512]{1,0:T(8,128)(2,1)S(1)} %collective-permute-done), channel_id=1, source_target_pairs={{0,4},{4,8},{8,12},{12,0},{1,5},{5,9},{9,13},{13,1},{2,6},{6,10},{... | collective-permute-start | bytes 3145736 | tf_op jit(solution)/shard_map/ppermute | solution.py:38
  38.4 22.6 %all-to-all-start = ((s32[64,1,16]{2,1,0:T(1,128)}), s32[64,1,16]{2,1,0:T(1,128)S(1)}, u32[]{:S(2)}, u32[]{:S(2)}) async-start(s32[64,1,16]{2,1,0:T(1,128)} %bitcast.2), calls=%async_computation | async-start | bytes 65536 | tf_op jit(solution)/shard_map/all_to_all | solution.py:45
  90.2 104.5 %all-to-all-start.1 = ((bf16[64,16,2048]{2,1,0:T(8,128)(2,1)}), bf16[64,16,2048]{2,1,0:T(8,128)(2,1)}, u32[]{:S(2)}, u32[]{:S(2)}) async-start(bf16[64,16,2048]{2,1,0:T(8,128)(2,1)} %broadcast_select_fusion), calls=%async_computation.1 | async-start | bytes 8388608 | tf_op jit(solution)/shard_map/all_to_all | solution.py:47
  101.2 141.6 %all-gather.3.cloned.1.call-start = ((), (), s32[]{:S(2)}) async-start(), calls=%async_computation.7 | async-start | bytes 1114112 | tf_op jit(solution)/shard_map/all_gather | solution.py:52
  203.8 3.8 copy-start.1
  207.5 94.8 %reduce-scatter.3.cloned.1.call-start = ((), (), s32[]{:S(2)}) async-start(), calls=%async_computation.5 | async-start | bytes 2228224 | tf_op jit(solution)/shard_map/reduce_scatter | solution.py:82
  317.8 104.5 %all-to-all-start.2 = ((bf16[64,16,2048]{2,1,0:T(8,128)(2,1)}), bf16[64,16,2048]{2,1,0:T(8,128)(2,1)}, u32[]{:S(2)}, u32[]{:S(2)}) async-start(bf16[64,16,2048]{2,1,0:T(8,128)(2,1)} %bitcast.56), calls=%async_computation.3 | async-start | bytes 8388608 | tf_op jit(solution)/shard_map/all_to_all | solution.py:94
  328.8 193.7 %reduce-scatter.5.cloned.1.call-start = ((), (), s32[]{:S(2)}) async-start(), calls=%async_computation.6 | async-start | bytes 10485760 | tf_op jit(solution)/shard_map/reduce_scatter | solution.py:99
  440.7 2.9 copy-start
Sparse Core Ops, SparseCore 0:
  207.6 35.1 all-gather.2
  246.8 55.3 reduce-scatter.2
  440.8 81.6 reduce-scatter.4
